TPU v7x, 128 devices: a whole 4x4x4 slice. The times are simulated.
128 devices in a mesh: ctx: 32 (over z, x, core), exp: 4 (over y).
Axes of the slice: x: 4, y: 4, z: 4, core: 2. Of those that a mesh axis runs over, the one named last changes fastest.
Arguments:
- queries: bfloat16 [8192, 4096], P('ctx', 'exp'), may hold values from -6 to 6
- key_rows: bfloat16 [8192, 4096], P('ctx', 'exp'), may hold values from -6 to 6
- value_rows: bfloat16 [8192, 4096], P('ctx', 'exp'), may hold values from -6 to 6
- gate_rows: bfloat16 [8192, 4096], P('ctx', 'exp'), may hold values from -6 to 6
- decay_exp: int32 [32], P('exp'), may hold values from 5 to 16
- attn_gain: float32 [4096], P('exp'), may hold values from 0.1 to 1.9
- out_proj: bfloat16 [4096, 6144], P('exp'), may hold values from -0.09375 to 0.09375
- residual: bfloat16 [8192, 6144], P(('ctx', 'exp')), may hold values from -6 to 6
- norm_gain: float32 [6144], replicated, may hold values from 0.1 to 1.9
- routes: int32 [8192, 2], P('ctx'), may hold values from 0 to 31, as said below
- route_weights: float32 [8192, 2], P('ctx'), may hold values from 0.1 to 1
- w_gate: bfloat16 [4, 9216, 6144], P('exp', 'ctx'), may hold values from -0.078125 to 0.078125
- w_up: bfloat16 [4, 9216, 6144], P('exp', 'ctx'), may hold values from -0.078125 to 0.078125
- w_down: bfloat16 [4, 9216, 6144], P('exp', 'ctx'), may hold values from -0.0625 to 0.0625
Outputs:
- layer_out: bfloat16 [8192, 6144], P(('ctx', 'exp'))
Inputs may be any that keep to these rules, and one draw needn't show every extreme that they name: `routes`: A row's two entries differ. An expert e below 4 is named only in column e % 2. In every aligned block of 64 rows each expert below 4 is named at most 8 times, and some expert below 4 exactly 8 times.
All inputs are finite; a program needn't handle non-finite values.
Results may differ from a plain program's by a relative error of at most 0.018.
Values may be sent and summed in bfloat16 or wider, within the bound.
A program may use at most 128 MiB of HBM per device.

v0:
```python
import jax
import jax.numpy as jnp
from jax import lax
from jax.sharding import PartitionSpec as P

EPSILON = 1e-06


def prefix(shard, axis, combine, identity):
    size, index = (lax.axis_size(axis), lax.axis_index(axis))
    everything = jax.tree.map(
        lambda part, kind: lax.all_gather(part.astype(kind), axis),
        shard,
        (jnp.bfloat16, jnp.bfloat16),
    )
    start = jax.tree.map(
        lambda part, zero: jnp.broadcast_to(jnp.asarray(zero, part.dtype), part.shape),
        shard,
        identity,
    )

    def turn(k, before):
        reached = k < index
        new = combine(
            before, jax.tree.map(lambda part, own: part[k].astype(own.dtype), everything, shard)
        )
        return jax.tree.map(lambda a, b: jnp.where(reached, a, b), new, before)

    return lax.fori_loop(0, size, turn, start)


def span_local(queries, key_rows, value_rows, decay_exp):
    row_count = queries.shape[0]
    head_count = decay_exp.shape[0]
    head_width = queries.shape[1] // head_count
    query_heads = queries.reshape(row_count, head_count, head_width)
    key_heads = key_rows.reshape(row_count, head_count, head_width)
    value_heads = value_rows.reshape(row_count, head_count, head_width)
    decay_rates = jnp.exp2(-decay_exp.astype(jnp.float32))
    positions = jnp.arange(row_count, dtype=jnp.float32)
    offsets = positions[:, None] - positions[None, :]
    damping = jnp.where(
        offsets[None] >= 0.0,
        jnp.exp(-decay_rates[:, None, None] * jnp.maximum(offsets, 0.0)[None]),
        0.0,
    )
    scores = jnp.einsum("thd,shd->hts", query_heads, key_heads, preferred_element_type=jnp.float32)
    mixing = (scores * damping).astype(jnp.bfloat16)
    inner_part = jnp.einsum("hts,shd->thd", mixing, value_heads, preferred_element_type=jnp.float32)
    tail_decay = jnp.exp(-decay_rates[None, :] * (row_count - 1.0 - positions)[:, None])
    keyed_rows = (key_heads.astype(jnp.float32) * tail_decay[:, :, None]).astype(jnp.bfloat16)
    update = jnp.einsum("shd,she->hde", keyed_rows, value_heads, preferred_element_type=jnp.float32)
    carry_decay = jnp.exp(-decay_rates * row_count)
    lead_decay = jnp.exp(-decay_rates[None, :] * (positions + 1.0)[:, None])
    leading = query_heads.astype(jnp.float32) * lead_decay[:, :, None]
    return (inner_part, leading, update, carry_decay)


def join_states(earlier, later):
    return (earlier[0] * later[0], later[0][:, None, None] * earlier[1] + later[1])


def settle(inner_part, leading, prior_state, gate_rows, attn_gain):
    outer_part = jnp.einsum("thd,hde->the", leading, prior_state, precision=lax.Precision.HIGHEST)
    mixed_heads = inner_part + outer_part
    row_count, head_count, head_width = mixed_heads.shape
    mean_square = jnp.mean(mixed_heads * mixed_heads, axis=2, keepdims=True)
    normed_heads = mixed_heads * lax.rsqrt(mean_square + EPSILON)
    gain_heads = attn_gain.reshape(head_count, head_width)
    gate_heads = gate_rows.reshape(row_count, head_count, head_width).astype(jnp.float32)
    settled = (normed_heads * gain_heads * jax.nn.sigmoid(gate_heads)).astype(jnp.bfloat16)
    return settled.reshape(row_count, head_count * head_width)


def token_norm(hidden, norm_gain):
    mean_square = jnp.mean(hidden * hidden, axis=1, keepdims=True)
    return (hidden * lax.rsqrt(mean_square + EPSILON) * norm_gain).astype(jnp.bfloat16)


def slot_tables(owners, chosen_ids, weights, capacity):
    column = owners % 2
    chosen = jnp.where(column[:, None] == 0, chosen_ids[None, :, 0], chosen_ids[None, :, 1])
    weight_rows = jnp.where(column[:, None] == 0, weights[None, :, 0], weights[None, :, 1])
    picked = chosen == owners[:, None]
    slot_rank = jnp.cumsum(picked.astype(jnp.int32), axis=1) - 1
    slot_ids = jnp.arange(capacity, dtype=jnp.int32)
    slot_table = picked[:, None, :] & (slot_rank[:, None, :] == slot_ids[None, :, None])
    return (slot_table.astype(jnp.bfloat16), jnp.where(slot_table, weight_rows[:, None, :], 0.0))


def expert_part(slot_rows, gate_cols, up_cols, down_rows):
    contract_dims = (((1,), (1,)), ((), ()))
    first_half = lax.dot_general(
        slot_rows, gate_cols, contract_dims, preferred_element_type=jnp.float32
    )
    second_half = lax.dot_general(
        slot_rows, up_cols, contract_dims, preferred_element_type=jnp.float32
    )
    activated = (jax.nn.silu(first_half) * second_half).astype(jnp.bfloat16)
    return jnp.dot(activated, down_rows, preferred_element_type=jnp.float32)


def body(
    queries,
    key_rows,
    value_rows,
    gate_rows,
    decay_exp,
    attn_gain,
    out_proj,
    residual,
    norm_gain,
    routes,
    route_weights,
    w_gate,
    w_up,
    w_down,
):
    inner_part, leading, update, carry_decay = span_local(queries, key_rows, value_rows, decay_exp)
    head_count = decay_exp.shape[0]
    head_width = queries.shape[1] // head_count
    identity = (
        jnp.ones((head_count,), jnp.float32),
        jnp.zeros((head_count, head_width, head_width), jnp.float32),
    )
    carried, prior_state = prefix((carry_decay, update), "ctx", join_states, identity)
    settled = settle(inner_part, leading, prior_state, gate_rows, attn_gain)
    span_rows = queries.shape[0]
    group_count = lax.axis_size("exp")
    group_rows = span_rows // group_count
    group_index = lax.axis_index("exp")
    first_mine = group_index * group_rows
    capacity = group_rows // 8
    gate_cols = w_gate[0]
    up_cols = w_up[0]
    down_rows = w_down[0]
    placed = lax.dynamic_update_slice_in_dim(
        jnp.zeros((span_rows, residual.shape[1]), jnp.float32),
        residual.astype(jnp.float32),
        first_mine,
        0,
    )
    projected = jnp.dot(settled, out_proj, preferred_element_type=jnp.float32) + placed
    hidden_all = lax.psum(projected.astype(jnp.bfloat16), "exp").astype(jnp.float32)
    normed_all = token_norm(hidden_all, norm_gain)
    owners = jnp.reshape(group_index, (1,))
    slot_table, weighted = slot_tables(owners, routes, route_weights, capacity * group_count)
    outgoing = jnp.einsum(
        "ecn,nd->cd", slot_table, normed_all, preferred_element_type=jnp.float32
    ).astype(jnp.bfloat16)
    gathered = lax.all_gather(outgoing, "ctx", axis=0, tiled=True)
    produced = lax.psum_scatter(
        expert_part(gathered, gate_cols, up_cols, down_rows).astype(jnp.bfloat16),
        "ctx",
        scatter_dimension=0,
        tiled=True,
    ).astype(jnp.float32)
    spread_back = jnp.einsum("ecn,cd->nd", weighted, produced, precision=lax.Precision.HIGHEST)
    mixture = lax.psum_scatter(
        spread_back.astype(jnp.bfloat16), "exp", scatter_dimension=0, tiled=True
    ).astype(jnp.float32)
    hidden = lax.dynamic_slice_in_dim(hidden_all, first_mine, group_rows, 0)
    return (hidden + mixture).astype(jnp.bfloat16)


def solution(mesh):
    in_specs = (
        P("ctx", "exp"),
        P("ctx", "exp"),
        P("ctx", "exp"),
        P("ctx", "exp"),
        P("exp"),
        P("exp"),
        P("exp", None),
        P(("ctx", "exp"), None),
        P(),
        P("ctx", None),
        P("ctx", None),
        P("exp", "ctx", None),
        P("exp", "ctx", None),
        P("exp", "ctx", None),
    )
    out_specs = P(("ctx", "exp"), None)
    return jax.shard_map(body, mesh=mesh, in_specs=in_specs, out_specs=out_specs, check_vma=False)
```

profile of v0, /device:TPU:1, one launch (start us, length us, event | category | flops | bytes accessed | tf_op | source)
XLA Modules:
  0.0 523.0 jit_solution(2067149946234657723)
XLA Ops:
  7.9 2.1 copy.36
  10.7 2.2 convolution_convert_fusion.3
  15.6 65.4 %all-reduce = bf16[256]{0:T(256)(128)(2,1)S(1)} all-reduce(bf16[256]{0:T(256)(128)(2,1)S(1)} %dynamic-update-slice.1), channel_id=2, replica_groups=mesh['ctx'=32,'exp'=4] {'ctx'}, use_global_device_ids=true, to_apply=%add | all-reduce | flops 256 | bytes 1024
  81.7 2.3 add_divide_fusion
  84.0 2.6 copy.34
  88.1 86.4 %while.14 = (s32[]{:T(128)}, f32[8,128,128]{2,1,0:T(8,128)}, s32[]{:T(128)}, bf16[32,8]{1,0:T(8,128)(2,1)}, bf16[32,8,128,128]{3,2,1,0:T(8,128)(2,1)}, /*index=5*/s32[]{:T(128)}, s32[]{:T(128)}) while((s32[]{:T(128)}, f32[8,128,128]{2,1,0:T(8,128)}, s32[]{:T(128)}, bf16[32,8]{1,0:T(8,128)(2,1)}, ...), condition=%wide.region_1.2_spmd.clone, body=%wide.region_0.1_spmd.clone.sunk | while | flops 655372 | bytes 1310905 | solution.py:29
  91.3 2.0 fusion.70
  94.1 2.0 fusion.70
  102.2 2.0 fusion.70
  174.5 3.6 convolution_bitcast_fusion
  178.1 3.7 multiply_reduce_fusion.1
  183.6 6.7 %fusion.57 = f32[256,6144]{1,0:T(8,128)S(1)} fusion(bf16[256,1024]{0,1:T(8,128)(2,1)S(1)} %bitcast.89, bf16[1024,6144]{1,0:T(8,128)(2,1)} %param.22), kind=kOutput, calls=%fused_computation.78 | convolution fusion | flops 3221225472 | bytes 19398656 | tf_op jit(solution)/shard_map/dot_general | solution.py:143
  190.6 2.1 convert_element_type.110
  193.5 76.0 %all-reduce.3.cloned.1.call-done = bf16[256,6144]{1,0:T(8,128)(2,1)} async-done(((bf16[256,6144]{1,0:T(8,128)(2,1)}), bf16[256,6144]{1,0:T(8,128)(2,1)}) %all-reduce.3.cloned.1.call-update) | async-done | bytes 3145744 | tf_op jit(solution)/shard_map/psum | solution.py:144
  269.6 2.6 multiply_reduce_fusion
  272.2 3.7 convolution_convert_fusion.2
  276.1 63.1 %all-gather.5.cloned.1.call-done = bf16[1024,6144]{1,0:T(8,128)(2,1)} async-done(((bf16[32,6144]{1,0:T(8,128)(2,1)}), bf16[1024,6144]{1,0:T(8,128)(2,1)}) %all-gather.5.cloned.1.call-update) | async-done | bytes 12582928 | tf_op jit(solution)/shard_map/all_gather | solution.py:151
  339.2 10.5 %fusion.4 = f32[1024,288]{0,1:T(8,128)} fusion(bf16[1024,6144]{1,0:T(8,128)(2,1)} %all-gather.5.cloned.1.call-done, bf16[1,288,6144]{2,1,0:T(8,128)(2,1)} %param.27), kind=kOutput, calls=%fused_computation.11 | convolution fusion | flops 3623878656 | bytes 17301504 | tf_op jit(solution)/shard_map/dot_general | solution.py:93
  349.7 17.7 %convolution_convert_fusion = bf16[1024,6144]{1,0:T(8,128)(2,1)} fusion(bf16[1,288,6144]{2,1,0:T(8,128)(2,1)S(1)} %copy-done, bf16[1024,6144]{1,0:T(8,128)(2,1)} %all-gather.5.cloned.1.call-done, bf16[1,288,6144]{2,1,0:T(8,128)(2,1)} %param.28, f32[1024,288]{0,1:T(8,128)} %fusion.4), kind=kOutput, calls=%fused_computation.3 | convolution fusion | flops 7255818240 | bytes 33423360 | tf_op jit(solution)/shard_map/dot_general | solution.py:100
  368.0 101.9 %reduce-scatter.3.cloned.1.call-done = bf16[32,6144]{1,0:T(8,128)(2,1)} async-done(((bf16[1024,6144]{1,0:T(8,128)(2,1)}), bf16[32,6144]{1,0:T(8,128)(2,1)}) %reduce-scatter.3.cloned.1.call-update) | async-done | bytes 393232 | tf_op jit(solution)/shard_map/reduce_scatter | solution.py:152
  469.9 5.1 convolution_convert_fusion.1
  475.1 5.4 %convert_element_type.111 = f32[256,6144]{1,0:T(8,128)} convert(bf16[256,6144]{1,0:T(8,128)(2,1)} %all-reduce.3.cloned.1.call-done) | non-fusion elementwise | flops 1572864 | bytes 9437184 | tf_op jit(solution)/shard_map/convert_element_type | solution.py:144
  480.5 33.3 %reduce-scatter.5.cloned.1.call-done = bf16[64,6144]{1,0:T(8,128)(2,1)} async-done(((bf16[256,6144]{1,0:T(8,128)(2,1)}), bf16[64,6144]{1,0:T(8,128)(2,1)}) %reduce-scatter.5.cloned.1.call-update) | async-done | bytes 786448 | tf_op jit(solution)/shard_map/reduce_scatter | solution.py:159
  513.8 2.7 add_convert_fusion
  (109 shorter events, 90.5 us)
Async XLA Ops:
  6.5 343.1 %copy-start = (bf16[1,288,6144]{2,1,0:T(8,128)(2,1)S(1)}, bf16[1,288,6144]{2,1,0:T(8,128)(2,1)}, u32[]{:S(2)}) copy-start(bf16[1,288,6144]{2,1,0:T(8,128)(2,1)} %param.29) | copy-start | bytes 10616836
  6.5 81.6 %all-gather.7.cloned.1.call-start = ((), (), s32[]{:S(2)}) async-start(), calls=%async_computation.6 | async-start | bytes 8650752 | tf_op jit(solution)/shard_map/all_gather | solution.py:12
  12.9 256.7 %all-reduce.3.cloned.1.call-start = ((), (), s32[]{:S(2)}) async-start(), calls=%async_computation.2 | async-start | bytes 6291456 | tf_op jit(solution)/shard_map/psum | solution.py:144
  88.1 90.0 %copy-start.6 = (f32[8]{0:T(128)S(1)}, f32[8]{0:T(128)}, u32[]{:S(2)}) copy-start(f32[8]{0:T(128)} %get-tuple-element.131) | copy-start | bytes 100
  174.5 7.3 %copy-start.3 = (f32[1024]{0:T(1024)S(1)}, f32[1024]{0:T(1024)}, u32[]{:S(2)}) copy-start(f32[1024]{0:T(1024)} %param.21) | copy-start | bytes 12292
  183.6 6.7 %copy-start.2 = (bf16[64,6144]{1,0:T(8,128)(2,1)S(1)}, bf16[64,6144]{1,0:T(8,128)(2,1)}, u32[]{:S(2)}) copy-start(bf16[64,6144]{1,0:T(8,128)(2,1)} %param.23) | copy-start | bytes 2359300
  190.6 2.2 copy-start.5
  192.7 146.5 %all-gather.5.cloned.1.call-start = ((), (), s32[]{:S(2)}) async-start(), calls=%async_computation.3 | async-start | bytes 12976128 | tf_op jit(solution)/shard_map/all_gather | solution.py:151
  275.9 194.0 %reduce-scatter.3.cloned.1.call-start = ((), (), s32[]{:S(2)}) async-start(), calls=%async_computation.4 | async-start | bytes 12976128 | tf_op jit(solution)/shard_map/reduce_scatter | solution.py:152
  367.3 0.7 copy-start.4
  367.4 146.5 %reduce-scatter.5.cloned.1.call-start = ((), (), s32[]{:S(2)}) async-start(), calls=%async_computation.5 | async-start | bytes 3932160 | tf_op jit(solution)/shard_map/reduce_scatter | solution.py:159
  475.0 41.5 %copy-start.1 = (bf16[1,288,6144]{2,1,0:T(8,128)(2,1)S(1)}, bf16[1,288,6144]{2,1,0:T(8,128)(2,1)}, u32[]{:S(2)}) copy-start(bf16[1,288,6144]{2,1,0:T(8,128)(2,1)} %param.29) | copy-start | bytes 10616836
Sparse Core Ops, SparseCore 0:
  13.0 56.8 all-gather.6
  192.8 76.7 all-reduce.2
  276.0 63.1 all-gather.4
  367.5 102.3 reduce-scatter.2
  475.2 38.6 reduce-scatter.4
where the time goes:
time: 525 us; the launch traced here: 523 us
  waiting for transfers between devices  274 us (52%)
  other arithmetic  108 us (21%)
  blocking collectives  65.4 us (12%)
  matrix products  53 us (10%)
  between operations  13.8 us (3%)
  local copies, waits for them, and re-layouts  8.36 us (2%)
    reduce_scatter x1, waiting for transfers between devices, body(): lax.psum_scatter(expert_part(gathered, gate_cols, up_cols, down_rows).ast...  102 us
    psum x1, waiting for transfers between devices, body(): lax.psum(projected.astype(jnp.bfloat16), 'exp').astype(jnp.float32)  76 us
    unnamed x1, blocking collectives  65.4 us
    select_n x32, other arithmetic, turn(): return jax.tree.map(lambda a, b: jnp.where(reached, a, b), new, before)  65.1 us
    all_gather x1, waiting for transfers between devices, body(): gathered = lax.all_gather(outgoing, 'ctx', axis=0, tiled=True)  63.1 us
    reduce_scatter x1, waiting for transfers between devices, body(): lax.psum_scatter(spread_back.astype(jnp.bfloat16), 'exp', scatter_dimensi...  33.3 us
    convert_element_type x32, other arithmetic, turn(): part[k].astype(own.dtype)  21.3 us
    dot_general x1, matrix products, expert_part(): return jnp.dot(activated, down_rows, preferred_element_type=jnp.float32)  17.7 us
  transfers between devices with their start and end apart: 5, of which 4 were waited for; matrix products, arithmetic and copies ran while one was open for 3% of the time, Pallas kernels for 0%

commit v1 on v0

--- a/solution.py
+++ b/solution.py
@@ -2,6 +2,7 @@
 import jax.numpy as jnp
 from jax import lax
 from jax.sharding import PartitionSpec as P
+from jax.lax import all_gather
 
 EPSILON = 1e-06
 
@@ -141,7 +142,12 @@
         0,
     )
     projected = jnp.dot(settled, out_proj, preferred_element_type=jnp.float32) + placed
-    hidden_all = lax.psum(projected.astype(jnp.bfloat16), "exp").astype(jnp.float32)
+
+    def balance_boxes_over_axis(message, peer_axis):
+        fresh = jnp.sum(all_gather(message, peer_axis), 0)
+        return fresh
+
+    hidden_all = balance_boxes_over_axis(projected.astype(jnp.bfloat16), "exp").astype(jnp.float32)
     normed_all = token_norm(hidden_all, norm_gain)
     owners = jnp.reshape(group_index, (1,))
     slot_table, weighted = slot_tables(owners, routes, route_weights, capacity * group_count)

time: 525 us -> 579 us (1.10)
  waiting for transfers between devices: 274 us -> 319 us
  other arithmetic: 108 us -> 117 us
    all_gather x0 -> x1, waiting for transfers between devices: none -> 119 us  [balance_boxes_over_axis(): fresh = jnp.sum(all_gather(message, peer_axis), 0)]
    psum x1 -> x0, waiting for transfers between devices: 76 us -> none  [body(): lax.psum(projected.astype(jnp.bfloat16), 'exp').astype(jnp.float32)]
    reduce_sum x0 -> x1, other arithmetic: none -> 9.57 us  [balance_boxes_over_axis(): fresh = jnp.sum(all_gather(message, peer_axis), 0)]
where the time goes in v1:
time: 579 us; the launch traced here: 577 us
  waiting for transfers between devices  319 us (55%)
  other arithmetic  117 us (20%)
  blocking collectives  65.4 us (11%)
  matrix products  53 us (9%)
  between operations  13.8 us (2%)
  local copies, waits for them, and re-layouts  8.36 us (1%)
    all_gather x1, waiting for transfers between devices, balance_boxes_over_axis(): fresh = jnp.sum(all_gather(message, peer_axis), 0)  119 us
    reduce_scatter x1, waiting for transfers between devices, body(): lax.psum_scatter(expert_part(gathered, gate_cols, up_cols, down_rows).ast...  102 us
    unnamed x1, blocking collectives  65.4 us
    select_n x32, other arithmetic, turn(): return jax.tree.map(lambda a, b: jnp.where(reached, a, b), new, before)  65.1 us
    all_gather x1, waiting for transfers between devices, body(): gathered = lax.all_gather(outgoing, 'ctx', axis=0, tiled=True)  64.3 us
    reduce_scatter x1, waiting for transfers between devices, body(): lax.psum_scatter(spread_back.astype(jnp.bfloat16), 'exp', scatter_dimensi...  33.4 us
    convert_element_type x32, other arithmetic, turn(): part[k].astype(own.dtype)  21.3 us
    dot_general x1, matrix products, expert_part(): return jnp.dot(activated, down_rows, preferred_element_type=jnp.float32)  17.7 us
  transfers between devices with their start and end apart: 5, of which 4 were waited for; matrix products, arithmetic and copies ran while one was open for 3% of the time, Pallas kernels for 0%

profile of v1, /device:TPU:1, one launch (start us, length us, event | category | flops | bytes accessed | tf_op | source)
XLA Modules:
  0.0 576.8 jit_solution(9405775109052293692)
XLA Ops:
  7.9 2.1 copy.36
  10.8 2.2 convolution_convert_fusion.3
  15.7 65.4 %all-reduce = bf16[256]{0:T(256)(128)(2,1)S(1)} all-reduce(bf16[256]{0:T(256)(128)(2,1)S(1)} %dynamic-update-slice.1), channel_id=2, replica_groups=mesh['ctx'=32,'exp'=4] {'ctx'}, use_global_device_ids=true, to_apply=%add | all-reduce | flops 256 | bytes 1024
  81.8 2.3 add_divide_fusion
  84.1 2.6 copy.34
  88.2 86.4 %while.14 = (s32[]{:T(128)}, f32[8,128,128]{2,1,0:T(8,128)}, s32[]{:T(128)}, bf16[32,8]{1,0:T(8,128)(2,1)}, bf16[32,8,128,128]{3,2,1,0:T(8,128)(2,1)}, /*index=5*/s32[]{:T(128)}, s32[]{:T(128)}) while((s32[]{:T(128)}, f32[8,128,128]{2,1,0:T(8,128)}, s32[]{:T(128)}, bf16[32,8]{1,0:T(8,128)(2,1)}, ...), condition=%wide.region_1.2_spmd.clone, body=%wide.region_0.1_spmd.clone.sunk | while | flops 655372 | bytes 1310905 | solution.py:30
  91.4 2.0 fusion.70
  102.3 2.0 fusion.70
  174.6 3.6 convolution_bitcast_fusion
  178.2 3.7 multiply_reduce_fusion.1
  183.7 6.7 %fusion.57 = f32[256,6144]{1,0:T(8,128)S(1)} fusion(bf16[256,1024]{0,1:T(8,128)(2,1)S(1)} %bitcast.91, bf16[1024,6144]{1,0:T(8,128)(2,1)} %param.22), kind=kOutput, calls=%fused_computation.78 | convolution fusion | flops 3221225472 | bytes 19398656 | tf_op jit(solution)/shard_map/dot_general | solution.py:144
  190.7 2.1 convert_element_type.112
  193.6 118.9 %all-gather.11.cloned.1.call-done = bf16[1024,6144]{1,0:T(8,128)(2,1)} async-done(((bf16[256,6144]{1,0:T(8,128)(2,1)}), bf16[1024,6144]{1,0:T(8,128)(2,1)}) %all-gather.11.cloned.1.call-update) | async-done | bytes 12582928 | tf_op jit(solution)/shard_map/all_gather | solution.py:147
  312.6 9.6 %reduce_sum.34 = bf16[256,6144]{1,0:T(8,128)(2,1)} reduce(bf16[4,256,6144]{2,1,0:T(8,128)(2,1)} %bitcast.89, bf16[]{:T(256)} %constant.86.clone.1), dimensions={0}, to_apply=%region_3.4 | reduce | flops 4718592 | bytes 15728642 | tf_op jit(solution)/shard_map/reduce_sum | solution.py:147
  322.1 2.6 multiply_reduce_fusion
  324.7 3.7 convolution_convert_fusion.2
  328.6 64.3 %all-gather.7.cloned.1.call-done = bf16[1024,6144]{1,0:T(8,128)(2,1)} async-done(((bf16[32,6144]{1,0:T(8,128)(2,1)}), bf16[1024,6144]{1,0:T(8,128)(2,1)}) %all-gather.7.cloned.1.call-update) | async-done | bytes 12582928 | tf_op jit(solution)/shard_map/all_gather | solution.py:157
  392.9 10.5 %fusion.4 = f32[1024,288]{0,1:T(8,128)} fusion(bf16[1024,6144]{1,0:T(8,128)(2,1)} %all-gather.7.cloned.1.call-done, bf16[1,288,6144]{2,1,0:T(8,128)(2,1)} %param.27), kind=kOutput, calls=%fused_computation.11 | convolution fusion | flops 3623878656 | bytes 17301504 | tf_op jit(solution)/shard_map/dot_general | solution.py:94
  403.4 17.7 %convolution_convert_fusion = bf16[1024,6144]{1,0:T(8,128)(2,1)} fusion(bf16[1,288,6144]{2,1,0:T(8,128)(2,1)S(1)} %copy-done, bf16[1024,6144]{1,0:T(8,128)(2,1)} %all-gather.7.cloned.1.call-done, bf16[1,288,6144]{2,1,0:T(8,128)(2,1)} %param.28, f32[1024,288]{0,1:T(8,128)} %fusion.4), kind=kOutput, calls=%fused_computation.3 | convolution fusion | flops 7255818240 | bytes 33423360 | tf_op jit(solution)/shard_map/dot_general | solution.py:101
  421.7 101.9 %reduce-scatter.3.cloned.1.call-done = bf16[32,6144]{1,0:T(8,128)(2,1)} async-done(((bf16[1024,6144]{1,0:T(8,128)(2,1)}), bf16[32,6144]{1,0:T(8,128)(2,1)}) %reduce-scatter.3.cloned.1.call-update) | async-done | bytes 393232 | tf_op jit(solution)/shard_map/reduce_scatter | solution.py:158
  523.6 5.1 convolution_convert_fusion.1
  528.8 5.4 convert_element_type.113
  534.2 33.4 %reduce-scatter.5.cloned.1.call-done = bf16[64,6144]{1,0:T(8,128)(2,1)} async-done(((bf16[256,6144]{1,0:T(8,128)(2,1)}), bf16[64,6144]{1,0:T(8,128)(2,1)}) %reduce-scatter.5.cloned.1.call-update) | async-done | bytes 786448 | tf_op jit(solution)/shard_map/reduce_scatter | solution.py:165
  567.6 2.7 add_convert_fusion
  (110 shorter events, 92.6 us)
Async XLA Ops:
  6.5 396.8 %copy-start = (bf16[1,288,6144]{2,1,0:T(8,128)(2,1)S(1)}, bf16[1,288,6144]{2,1,0:T(8,128)(2,1)}, u32[]{:S(2)}) copy-start(bf16[1,288,6144]{2,1,0:T(8,128)(2,1)} %param.29) | copy-start | bytes 10616836
  6.5 81.6 %all-gather.9.cloned.1.call-start = ((), (), s32[]{:S(2)}) async-start(), calls=%async_computation.5 | async-start | bytes 8650752 | tf_op jit(solution)/shard_map/all_gather | solution.py:13
  13.0 299.6 %all-gather.11.cloned.1.call-start = ((), (), s32[]{:S(2)}) async-start(), calls=%async_computation.6 | async-start | bytes 15728640 | tf_op jit(solution)/shard_map/all_gather | solution.py:147
  88.2 90.0 %copy-start.6 = (f32[8]{0:T(128)S(1)}, f32[8]{0:T(128)}, u32[]{:S(2)}) copy-start(f32[8]{0:T(128)} %get-tuple-element.131) | copy-start | bytes 100
  174.6 7.3 %copy-start.3 = (f32[1024]{0:T(1024)S(1)}, f32[1024]{0:T(1024)}, u32[]{:S(2)}) copy-start(f32[1024]{0:T(1024)} %param.21) | copy-start | bytes 12292
  183.7 6.7 %copy-start.2 = (bf16[64,6144]{1,0:T(8,128)(2,1)S(1)}, bf16[64,6144]{1,0:T(8,128)(2,1)}, u32[]{:S(2)}) copy-start(bf16[64,6144]{1,0:T(8,128)(2,1)} %param.23) | copy-start | bytes 2359300
  190.7 2.2 copy-start.5
  192.8 200.1 %all-gather.7.cloned.1.call-start = ((), (), s32[]{:S(2)}) async-start(), calls=%async_computation.2 | async-start | bytes 12976128 | tf_op jit(solution)/shard_map/all_gather | solution.py:157
  328.4 195.2 %reduce-scatter.3.cloned.1.call-start = ((), (), s32[]{:S(2)}) async-start(), calls=%async_computation.3 | async-start | bytes 12976128 | tf_op jit(solution)/shard_map/reduce_scatter | solution.py:158
  421.0 0.7 copy-start.4
  421.1 146.5 %reduce-scatter.5.cloned.1.call-start = ((), (), s32[]{:S(2)}) async-start(), calls=%async_computation.4 | async-start | bytes 3932160 | tf_op jit(solution)/shard_map/reduce_scatter | solution.py:165
  528.7 41.5 %copy-start.1 = (bf16[1,288,6144]{2,1,0:T(8,128)(2,1)S(1)}, bf16[1,288,6144]{2,1,0:T(8,128)(2,1)}, u32[]{:S(2)}) copy-start(bf16[1,288,6144]{2,1,0:T(8,128)(2,1)} %param.29) | copy-start | bytes 10616836
Sparse Core Ops, SparseCore 0:
  13.1 56.8 all-gather.8
  192.9 119.6 all-gather.10
  328.5 64.3 all-gather.6
  421.2 102.3 reduce-scatter.2
  528.9 38.6 reduce-scatter.4
